TPU v7x, 32 devices: a whole 2x2x4 slice. The times are simulated.
32 devices in a mesh: blocks: 2 (over y), rows: 4 (over z), cols: 4 (over x, core).
Axes of the slice: x: 2, y: 2, z: 4, core: 2. Of those that a mesh axis runs over, the one named last changes fastest.
Arguments:
- sens_tiles: bfloat16 [128, 1024, 256], P(('blocks', 'rows'), 'cols'), parts along dimension 0, may hold values from -10.606602 to 10.606602, as said below
- tile_coords: int32 [128, 8], P(('blocks', 'rows'), 'cols'), parts along dimension 0, may hold values from 0 to 7, as said below
- tile_counts: int32 [8, 4], P(('blocks', 'rows'), 'cols'), parts along dimension 0, may hold values from 3 to 16, as said below
- data_vec: float32 [192, 4096], P('blocks', 'rows'), parts along dimension 0, may hold values from -6 to 6
- cell_vec: float32 [192, 8192], P('blocks', 'cols'), parts along dimension 0, may hold values from -6 to 6
- alpha_now: float32 [192], P('blocks'), parts along dimension 0, may hold values from 0.5 to 2
Outputs:
- data_next: float32 [192, 4096], P('blocks', 'rows'), parts along dimension 0
- cell_next: float32 [192, 8192], P('blocks', 'cols'), parts along dimension 0
- beta_next: float32 [192], P('blocks'), parts along dimension 0
- alpha_next: float32 [192], P('blocks'), parts along dimension 0
There are 2 independent parts, one for each index of `blocks`. A program takes and returns all parts, laid end to end along the dimension named above; each array names one. Nothing has to cross between parts.
Inputs may be any that keep to these rules, and one draw needn't show every extreme that they name: `sens_tiles`: entries of the tiles; slots at or beyond a device's count hold values that belong to no tile. `tile_coords`: within one device all 16 slots name distinct (row tile, column tile) pairs; the first entry of a pair is below 4, the second below 8. `tile_counts`: every data-row band has one device whose count is 16.
All inputs are finite; a program needn't handle non-finite values.
Results may differ from a plain program's by a relative error of at most 0.0043.
Values sent between devices are 32-bit elements; how exact they have to be, the bound alone decides.
No kernel may reach another device: no remote copies, remote signals or barrier semaphores. Data moves between devices by JAX's collectives and lax.ppermute only.
A program may use at most 64 MiB of HBM per device.

v0:
```python
import jax
import jax.numpy as jnp
from jax import lax
from jax.sharding import PartitionSpec as P

EPSILON = 1e-06


def listed_mask(sens_tiles, listed_count):
    return (jnp.arange(sens_tiles.shape[0], dtype=jnp.int32) < listed_count).astype(jnp.float32)


def forward_sweep(sens_tiles, tile_coords, listed_count, cell_low, row_tiles):
    samples = cell_low.shape[0]
    tile_size = sens_tiles.shape[1]
    listed = listed_mask(sens_tiles, listed_count)
    blocks = cell_low.reshape(samples, cell_low.shape[1] // tile_size, tile_size)
    picked = jnp.take(blocks, tile_coords[:, 1], axis=1)
    contrib = jnp.einsum("ktj,tij->kti", picked, sens_tiles, preferred_element_type=jnp.float32)
    spread = jax.nn.one_hot(tile_coords[:, 0], row_tiles, dtype=jnp.float32) * listed[:, None]
    placed = jnp.einsum("kti,tr->kri", contrib, spread, precision=lax.Precision.HIGHEST)
    return placed.reshape(samples, row_tiles * tile_size)


def adjoint_sweep(sens_tiles, tile_coords, listed_count, data_low, col_tiles):
    samples = data_low.shape[0]
    tile_size = sens_tiles.shape[1]
    listed = listed_mask(sens_tiles, listed_count)
    blocks = data_low.reshape(samples, data_low.shape[1] // tile_size, tile_size)
    picked = jnp.take(blocks, tile_coords[:, 0], axis=1)
    contrib = jnp.einsum("kti,tij->ktj", picked, sens_tiles, preferred_element_type=jnp.float32)
    spread = jax.nn.one_hot(tile_coords[:, 1], col_tiles, dtype=jnp.float32) * listed[:, None]
    placed = jnp.einsum("ktj,ts->ksj", contrib, spread, precision=lax.Precision.HIGHEST)
    return placed.reshape(samples, col_tiles * tile_size)


def per_device(sens_tiles, tile_coords, tile_counts, data_vec, cell_vec, alpha_now):
    tile_size = sens_tiles.shape[1]
    row_tiles = data_vec.shape[1] // tile_size
    col_tiles = cell_vec.shape[1] // tile_size
    listed_count = tile_counts[0, 0]
    data_total = data_vec.shape[1] * lax.axis_size("rows")
    cell_total = cell_vec.shape[1] * lax.axis_size("cols")
    cell_low = cell_vec.astype(jnp.bfloat16)
    partial_rows = forward_sweep(sens_tiles, tile_coords, listed_count, cell_low, row_tiles)
    row_full = lax.psum(partial_rows, "cols")
    residual = row_full - alpha_now[:, None] * data_vec
    squares = lax.psum(jnp.sum(residual * residual, axis=1), "rows")
    beta_next = jnp.sqrt(squares / data_total + EPSILON)
    data_next = residual / beta_next[:, None]
    data_low = data_next.astype(jnp.bfloat16)
    partial_cells = adjoint_sweep(sens_tiles, tile_coords, listed_count, data_low, col_tiles)
    cell_full = lax.psum(partial_cells, "rows")
    fresh = cell_full - beta_next[:, None] * cell_vec
    sumsq = lax.psum(jnp.sum(fresh * fresh, axis=1), "cols")
    alpha_next = jnp.sqrt(sumsq / cell_total + EPSILON)
    cell_next = fresh / alpha_next[:, None]
    return (data_next, cell_next, beta_next, alpha_next)


def solution(mesh):
    placed = (
        P(("blocks", "rows"), "cols", None),
        P(("blocks", "rows"), "cols"),
        P(("blocks", "rows"), "cols"),
        P("blocks", "rows"),
        P("blocks", "cols"),
        P("blocks"),
    )
    return jax.shard_map(
        per_device,
        mesh=mesh,
        in_specs=placed,
        out_specs=(P("blocks", "rows"), P("blocks", "cols"), P("blocks"), P("blocks")),
        check_vma=False,
    )
```

profile of v0, /device:TPU:0, one launch (start us, length us, event | category | flops | bytes accessed | tf_op | source)
XLA Modules:
  0.0 127.0 jit_solution(8777433551403314318)
XLA Ops:
  7.2 0.0 copy-start
  7.2 0.0 all-reduce.3.cloned.1.call-start
  7.2 0.8 and_bitcast_fusion
  8.1 0.8 slice_bitcast_fusion
  9.5 1.2 convert_element_type.19
  10.7 0.6 gather_fusion
  11.3 0.0 copy-done
  11.3 0.8 convolution_bitcast_fusion.1
  12.1 0.0 copy-start.2
  12.1 0.0 copy-start.4
  12.1 1.7 %fusion.2 = f32[4,96,256]{2,0,1:T(4,128)S(1)} fusion(f32[96,16,256]{2,0,1:T(8,128)S(1)} %convolution_bitcast_fusion.1, f32[16]{0:T(128)S(1)} %compare_convert_fusion, s32[16]{0:T(128)S(1)} %get-tuple-element.9), kind=kOutput, calls=%fused_computation.4 | convolution fusion | flops 18874496 | bytes 1966208 | tf_op jit(solution)/shard_map/kti,tr->kri/dot_general | solution.py:21
  13.9 0.8 copy.16
  14.7 0.0 all-reduce.3.cloned.1.call-update
  14.7 0.0 all-reduce.5.cloned.1.call-start
  14.8 35.6 %all-reduce.3.cloned.1.call-done = f32[96,1024]{1,0:T(8,128)} async-done(((f32[96,1024]{1,0:T(8,128)}), f32[96,1024]{1,0:T(8,128)}) %all-reduce.3.cloned.1.call-update) | async-done | bytes 393232 | tf_op jit(solution)/shard_map/psum | solution.py:46
  50.4 0.0 copy-done.2
  50.4 0.0 copy-done.4
  50.4 1.2 multiply_reduce_fusion.1
  51.6 11.7 %psum.29 = f32[96]{0:T(128)S(1)} all-reduce(f32[96]{0:T(128)S(1)} %multiply_reduce_fusion.1), channel_id=1, replica_groups=mesh['blocks'=2,'rows'=4,'cols'=4] {'rows'}, use_global_device_ids=true, to_apply=%region_2.3 | all-reduce | flops 96 | bytes 768 | tf_op jit(solution)/shard_map/psum | solution.py:48
  63.3 0.0 copy-start.3
  63.3 1.9 %fusion.28 = (bf16[96,1024]{1,0:T(8,128)(2,1)S(1)}, f32[96,1024]{1,0:T(8,128)}) fusion(f32[96]{0:T(128)S(1)} %add_sqrt_fusion.1, f32[96,1024]{1,0:T(8,128)} %all-reduce.3.cloned.1.call-done, f32[96,1024]{1,0:T(8,128)S(1)} %copy-done.2, f32[96]{0:T(128)S(1)} %copy-done.4), kind=kLoop, calls=%fused_computation.53 | loop fusion | flops 393216 | bytes 1377024 | tf_op jit(solution)/shard_map/convert_element_type | solution.py:51
  65.2 0.6 gather_fusion.1
  65.8 0.5 convolution_bitcast_fusion
  66.3 1.7 %fusion = f32[8,96,256]{2,0,1:T(8,128)S(1)} fusion(f32[96,16,256]{2,0,1:T(8,128)S(1)} %convolution_bitcast_fusion, f32[16]{0:T(128)S(1)} %compare_convert_fusion, s32[16]{0:T(128)S(1)} %get-tuple-element.6), kind=kOutput, calls=%fused_computation.2 | convolution fusion | flops 37748992 | bytes 2359424 | tf_op jit(solution)/shard_map/ktj,ts->ksj/dot_general | solution.py:33
  68.1 0.0 copy-start.1
  68.1 1.1 copy.17
  69.2 0.0 all-reduce.5.cloned.1.call-update
  69.2 41.3 %all-reduce.5.cloned.1.call-done = f32[96,2048]{1,0:T(8,128)} async-done(((f32[96,2048]{1,0:T(8,128)}), f32[96,2048]{1,0:T(8,128)}) %all-reduce.5.cloned.1.call-update) | async-done | bytes 786448 | tf_op jit(solution)/shard_map/psum | solution.py:53
  110.5 0.0 copy-done.1
  110.5 1.4 %multiply_reduce_fusion = f32[96]{0:T(128)S(1)} fusion(f32[96,2048]{1,0:T(8,128)} %all-reduce.5.cloned.1.call-done, f32[96,2048]{1,0:T(8,128)S(1)} %copy-done.1, f32[96]{0:T(128)S(1)} %add_sqrt_fusion.1), kind=kLoop, calls=%fused_computation.12 | loop fusion | flops 786336 | bytes 1573632 | tf_op jit(solution)/shard_map/reduce_sum | solution.py:55
  111.9 6.0 %psum.31 = f32[96]{0:T(128)S(1)} all-reduce(f32[96]{0:T(128)S(1)} %multiply_reduce_fusion), channel_id=1, replica_groups=mesh['blocks'=2,'rows'=4,'cols'=4] {'cols'}, use_global_device_ids=true, to_apply=%region_5.6 | all-reduce | flops 96 | bytes 768 | tf_op jit(solution)/shard_map/psum | solution.py:55
  118.0 0.0 copy-done.3
  118.0 0.0 copy-start.5
  118.0 2.2 %broadcast_divide_fusion = f32[96,2048]{1,0:T(8,128)} fusion(f32[96]{0:T(128)S(1)} %add_sqrt_fusion, f32[96,2048]{1,0:T(8,128)} %all-reduce.5.cloned.1.call-done, f32[96,2048]{1,0:T(8,128)S(1)} %copy-done.1, f32[96]{0:T(128)S(1)} %add_sqrt_fusion.1), kind=kLoop, calls=%fused_computation.19 | loop fusion | flops 589824 | bytes 2360064 | tf_op jit(solution)/shard_map/div | solution.py:57
  120.2 0.0 copy-done.5
  (6 shorter events, 0.1 us)
Async XLA Ops:
  7.2 4.2 %copy-start = (bf16[16,256,256]{2,1,0:T(8,128)(2,1)S(1)}, bf16[16,256,256]{2,1,0:T(8,128)(2,1)}, u32[]{:S(2)}) copy-start(bf16[16,256,256]{2,1,0:T(8,128)(2,1)} %param.6) | copy-start | bytes 6291460
  7.2 43.2 %all-reduce.3.cloned.1.call-start = ((), (), s32[]{:S(2)}) async-start(), calls=%async_computation | async-start | bytes 786432 | tf_op jit(solution)/shard_map/psum | solution.py:46
  12.1 38.3 %copy-start.2 = (f32[96,1024]{1,0:T(8,128)S(1)}, f32[96,1024]{1,0:T(8,128)}, u32[]{:S(2)}) copy-start(f32[96,1024]{1,0:T(8,128)} %param.9) | copy-start | bytes 1179652
  12.1 38.3 %copy-start.4 = (f32[96]{0:T(128)S(1)}, f32[96]{0:T(128)}, u32[]{:S(2)}) copy-start(f32[96]{0:T(128)} %param.11) | copy-start | bytes 1156
  14.7 95.8 %all-reduce.5.cloned.1.call-start = ((), (), s32[]{:S(2)}) async-start(), calls=%async_computation.1 | async-start | bytes 1572864 | tf_op jit(solution)/shard_map/psum | solution.py:53
  63.3 54.7 %copy-start.3 = (f32[96]{0:T(128)}, f32[96]{0:T(128)S(1)}, u32[]{:S(2)}) copy-start(f32[96]{0:T(128)S(1)} %add_sqrt_fusion.1) | copy-start | bytes 1156
  68.1 42.5 %copy-start.1 = (f32[96,2048]{1,0:T(8,128)S(1)}, f32[96,2048]{1,0:T(8,128)}, u32[]{:S(2)}) copy-start(f32[96,2048]{1,0:T(8,128)} %param.10) | copy-start | bytes 2359300
  118.0 2.2 %copy-start.5 = (f32[96]{0:T(128)}, f32[96]{0:T(128)S(1)}, u32[]{:S(2)}) copy-start(f32[96]{0:T(128)S(1)} %add_sqrt_fusion) | copy-start | bytes 1156
Sparse Core Ops, SparseCore 0:
  14.8 35.5 all-reduce.2
  69.3 41.1 all-reduce.4
where the time goes:
time: 127 us
  waiting for transfers between devices  77 us (61%)
  blocking collectives  17.7 us (14%)
  between operations  14.8 us (12%)
  other arithmetic  9.5 us (7%)
  matrix products  4.7 us (4%)
  local copies, waits for them, and re-layouts  3.22 us (3%)
    psum x1, waiting for transfers between devices, per_device(): cell_full = lax.psum(partial_cells, 'rows')  41.3 us
    psum x1, waiting for transfers between devices, per_device(): row_full = lax.psum(partial_rows, 'cols')  35.6 us
    psum x1, blocking collectives, per_device(): squares = lax.psum(jnp.sum(residual * residual, axis=1), 'rows')  11.7 us
    psum x1, blocking collectives, per_device(): sumsq = lax.psum(jnp.sum(fresh * fresh, axis=1), 'cols')  6.04 us
  transfers between devices with their start and end apart: 2, of which 2 were waited for; matrix products, arithmetic and copies ran while one was open for 0% of the time, Pallas kernels for 0%

commit v1 on v0

--- a/solution.py
+++ b/solution.py
@@ -2,6 +2,7 @@
 import jax.numpy as jnp
 from jax import lax
 from jax.sharding import PartitionSpec as P
+from jax.lax import all_gather
 
 EPSILON = 1e-06
 
@@ -50,7 +51,7 @@
     data_next = residual / beta_next[:, None]
     data_low = data_next.astype(jnp.bfloat16)
     partial_cells = adjoint_sweep(sens_tiles, tile_coords, listed_count, data_low, col_tiles)
-    cell_full = lax.psum(partial_cells, "rows")
+    cell_full = jnp.sum(all_gather(partial_cells, axis_name="rows"), axis=0)
     fresh = cell_full - beta_next[:, None] * cell_vec
     sumsq = lax.psum(jnp.sum(fresh * fresh, axis=1), "cols")
     alpha_next = jnp.sqrt(sumsq / cell_total + EPSILON)

time: 127 us -> 150 us (1.18)
  waiting for transfers between devices: 77 us -> 96.5 us
  other arithmetic: 9.5 us -> 12.6 us
    all_gather x0 -> x1, waiting for transfers between devices: none -> 60.8 us  [per_device(): cell_full = jnp.sum(all_gather(partial_cells, axis_name='rows'), axis=0)]
    psum x1 -> x0, waiting for transfers between devices: 41.3 us -> none  [per_device(): cell_full = lax.psum(partial_cells, 'rows')]
    reduce_sum x0 -> x1, other arithmetic: none -> 3.05 us  [per_device(): cell_full = jnp.sum(all_gather(partial_cells, axis_name='rows'), axis=0)]
where the time goes in v1:
time: 150 us
  waiting for transfers between devices  96.5 us (64%)
  blocking collectives  18.1 us (12%)
  between operations  14.8 us (10%)
  other arithmetic  12.6 us (8%)
  matrix products  4.7 us (3%)
  local copies, waits for them, and re-layouts  3.09 us (2%)
    all_gather x1, waiting for transfers between devices, per_device(): cell_full = jnp.sum(all_gather(partial_cells, axis_name='rows'), axis=0)  60.8 us
    psum x1, waiting for transfers between devices, per_device(): row_full = lax.psum(partial_rows, 'cols')  35.6 us
    psum x1, blocking collectives, per_device(): squares = lax.psum(jnp.sum(residual * residual, axis=1), 'rows')  11.7 us
    psum x1, blocking collectives, per_device(): sumsq = lax.psum(jnp.sum(fresh * fresh, axis=1), 'cols')  6.4 us
    reduce_sum x1, other arithmetic, per_device(): cell_full = jnp.sum(all_gather(partial_cells, axis_name='rows'), axis=0)  3.05 us
  transfers between devices with their start and end apart: 2, of which 2 were waited for; matrix products, arithmetic and copies ran while one was open for 0% of the time, Pallas kernels for 0%

profile of v1, /device:TPU:0, one launch (start us, length us, event | category | flops | bytes accessed | tf_op | source)
XLA Modules:
  0.0 149.8 jit_solution(15041443913796763184)
XLA Ops:
  7.2 0.0 copy-start
  7.2 0.0 all-reduce.2.cloned.1.call-start
  7.2 0.8 and_bitcast_fusion
  8.1 0.8 slice_bitcast_fusion
  9.5 1.2 convert_element_type.19
  10.7 0.6 gather_fusion
  11.3 0.0 copy-done
  11.3 0.8 convolution_bitcast_fusion.1
  12.1 0.0 copy-start.2
  12.1 0.0 copy-start.4
  12.1 1.7 %fusion.2 = f32[4,96,256]{2,0,1:T(4,128)S(1)} fusion(f32[96,16,256]{2,0,1:T(8,128)S(1)} %convolution_bitcast_fusion.1, f32[16]{0:T(128)S(1)} %compare_convert_fusion, s32[16]{0:T(128)S(1)} %get-tuple-element.9), kind=kOutput, calls=%fused_computation.4 | convolution fusion | flops 18874496 | bytes 1966208 | tf_op jit(solution)/shard_map/kti,tr->kri/dot_general | solution.py:22
  13.9 0.8 copy.20
  14.7 0.0 all-reduce.2.cloned.1.call-update
  14.7 0.0 all-gather.2.cloned.1.call-start
  14.8 35.6 %all-reduce.2.cloned.1.call-done = f32[96,1024]{1,0:T(8,128)} async-done(((f32[96,1024]{1,0:T(8,128)}), f32[96,1024]{1,0:T(8,128)}) %all-reduce.2.cloned.1.call-update) | async-done | bytes 393232 | tf_op jit(solution)/shard_map/psum | solution.py:47
  50.4 0.0 copy-done.2
  50.4 0.0 copy-done.4
  50.4 1.2 multiply_reduce_fusion.1
  51.6 11.7 %psum.22 = f32[96]{0:T(128)S(1)} all-reduce(f32[96]{0:T(128)S(1)} %multiply_reduce_fusion.1), channel_id=1, replica_groups=mesh['blocks'=2,'rows'=4,'cols'=4] {'rows'}, use_global_device_ids=true, to_apply=%region_2.3 | all-reduce | flops 96 | bytes 768 | tf_op jit(solution)/shard_map/psum | solution.py:49
  63.3 0.0 copy-start.3
  63.3 1.9 %fusion.31 = (bf16[96,1024]{1,0:T(8,128)(2,1)S(1)}, f32[96,1024]{1,0:T(8,128)}) fusion(f32[96]{0:T(128)S(1)} %add_sqrt_fusion.1, f32[96,1024]{1,0:T(8,128)} %all-reduce.2.cloned.1.call-done, f32[96,1024]{1,0:T(8,128)S(1)} %copy-done.2, f32[96]{0:T(128)S(1)} %copy-done.4), kind=kLoop, calls=%fused_computation.54 | loop fusion | flops 393216 | bytes 1377024 | tf_op jit(solution)/shard_map/convert_element_type | solution.py:52
  65.2 0.6 gather_fusion.1
  65.8 0.5 convolution_bitcast_fusion
  66.4 1.7 %fusion.4 = f32[96,8,256]{2,1,0:T(8,128)S(1)} fusion(f32[96,16,256]{2,0,1:T(8,128)S(1)} %convolution_bitcast_fusion, f32[16]{0:T(128)S(1)} %compare_convert_fusion, s32[16]{0:T(128)S(1)} %get-tuple-element.6), kind=kOutput, calls=%fused_computation.8 | convolution fusion | flops 37748992 | bytes 2359424 | tf_op jit(solution)/shard_map/ktj,ts->ksj/dot_general | solution.py:34
  68.1 1.0 all_gather_reshape.3
  69.1 0.0 all-gather.2.cloned.1.call-update
  69.1 0.0 copy-start.1
  69.1 60.8 %all-gather.2.cloned.1.call-done = f32[4,96,2048]{2,1,0:T(8,128)} async-done(((f32[1,96,2048]{2,1,0:T(8,128)}), f32[4,96,2048]{2,1,0:T(8,128)}) %all-gather.2.cloned.1.call-update) | async-done | bytes 3145744 | tf_op jit(solution)/shard_map/all_gather | solution.py:54
  129.9 3.1 %reduce_sum.28 = f32[96,2048]{1,0:T(8,128)} reduce(f32[4,96,2048]{2,1,0:T(8,128)} %all-gather.2.cloned.1.call-done, f32[]{:T(128)} %constant.32.clone.1), dimensions={0}, to_apply=%region_3.4 | reduce | flops 589824 | bytes 3932164 | tf_op jit(solution)/shard_map/reduce_sum | solution.py:54
  133.0 0.0 copy-done.1
  133.0 1.4 multiply_reduce_fusion
  134.4 6.4 %psum.23 = f32[96]{0:T(128)S(1)} all-reduce(f32[96]{0:T(128)S(1)} %multiply_reduce_fusion), channel_id=1, replica_groups=mesh['blocks'=2,'rows'=4,'cols'=4] {'cols'}, use_global_device_ids=true, to_apply=%region_5.6 | all-reduce | flops 96 | bytes 768 | tf_op jit(solution)/shard_map/psum | solution.py:56
  140.8 0.0 copy-done.3
  140.8 0.0 copy-start.5
  140.8 2.2 %broadcast_divide_fusion = f32[96,2048]{1,0:T(8,128)} fusion(f32[96]{0:T(128)S(1)} %add_sqrt_fusion, f32[96,2048]{1,0:T(8,128)} %reduce_sum.28, f32[96,2048]{1,0:T(8,128)S(1)} %copy-done.1, f32[96]{0:T(128)S(1)} %add_sqrt_fusion.1), kind=kLoop, calls=%fused_computation.20 | loop fusion | flops 589824 | bytes 2360064 | tf_op jit(solution)/shard_map/div | solution.py:58
  143.0 0.0 copy-done.5
  (6 shorter events, 0.1 us)
Async XLA Ops:
  7.2 4.2 %copy-start = (bf16[16,256,256]{2,1,0:T(8,128)(2,1)S(1)}, bf16[16,256,256]{2,1,0:T(8,128)(2,1)}, u32[]{:S(2)}) copy-start(bf16[16,256,256]{2,1,0:T(8,128)(2,1)} %param.6) | copy-start | bytes 6291460
  7.2 43.2 %all-reduce.2.cloned.1.call-start = ((), (), s32[]{:S(2)}) async-start(), calls=%async_computation | async-start | bytes 786432 | tf_op jit(solution)/shard_map/psum | solution.py:47
  12.1 38.3 %copy-start.2 = (f32[96,1024]{1,0:T(8,128)S(1)}, f32[96,1024]{1,0:T(8,128)}, u32[]{:S(2)}) copy-start(f32[96,1024]{1,0:T(8,128)} %param.9) | copy-start | bytes 1179652
  12.1 38.3 %copy-start.4 = (f32[96]{0:T(128)S(1)}, f32[96]{0:T(128)}, u32[]{:S(2)}) copy-start(f32[96]{0:T(128)} %param.11) | copy-start | bytes 1156
  14.7 115.2 %all-gather.2.cloned.1.call-start = ((), (), s32[]{:S(2)}) async-start(), calls=%async_computation.1 | async-start | bytes 3932160 | tf_op jit(solution)/shard_map/all_gather | solution.py:54
  63.3 77.5 %copy-start.3 = (f32[96]{0:T(128)}, f32[96]{0:T(128)S(1)}, u32[]{:S(2)}) copy-start(f32[96]{0:T(128)S(1)} %add_sqrt_fusion.1) | copy-start | bytes 1156
  69.1 63.9 %copy-start.1 = (f32[96,2048]{1,0:T(8,128)S(1)}, f32[96,2048]{1,0:T(8,128)}, u32[]{:S(2)}) copy-start(f32[96,2048]{1,0:T(8,128)} %param.10) | copy-start | bytes 2359300
  140.8 2.2 %copy-start.5 = (f32[96]{0:T(128)}, f32[96]{0:T(128)S(1)}, u32[]{:S(2)}) copy-start(f32[96]{0:T(128)S(1)} %add_sqrt_fusion) | copy-start | bytes 1156
Sparse Core Ops, SparseCore 0:
  14.8 35.5 all-reduce.1
  69.2 60.6 all-gather.1
